TPU v7x, 32 devices: a whole 2x2x4 slice. The times are simulated.
32 devices in a mesh: mem: 4 (over x, core), slab: 8 (over z, y).
Axes of the slice: x: 2, y: 2, z: 4, core: 2. Of those that a mesh axis runs over, the one named last changes fastest.
Arguments:
- anomalies: bfloat16 [8, 4096, 4096], P('mem', 'slab'), may hold values from -2.390625 to 2.390625
- increment: float32 [4096, 4096], P('slab'), may hold values from -6 to 6
- spectrum: float32 [4096, 4096], P(None, 'slab'), may hold values from 0.01 to 2, as said below
Outputs:
- product: float32 [4096, 4096], P('slab')
Inputs may be any that keep to these rules, and one draw needn't show every extreme that they name: spectrum[k, l] equals spectrum[(4096 - k) % 4096, (4096 - l) % 4096], and is positive.
All inputs are finite; a program needn't handle non-finite values.
Results may differ from a plain program's by a relative error of at most 0.0003.
Values sent between devices are 32-bit elements; how exact they have to be, the bound alone decides.
A program may use at most 192 MiB of HBM per device.

v0:
```python
import math

import jax
import jax.numpy as jnp
from jax import lax
from jax.sharding import PartitionSpec as P


def dft_tables(length, sign):
    first = 1 << (length.bit_length() - 1) // 2
    second = length // first
    index_a = jnp.arange(first, dtype=jnp.int32)
    index_b = jnp.arange(second, dtype=jnp.int32)
    angle_first = (
        2.0 * math.pi / first * (index_a[:, None] * index_a[None, :] % first).astype(jnp.float32)
    )
    angle_twist = (
        2.0 * math.pi / length * (index_a[:, None] * index_b[None, :] % length).astype(jnp.float32)
    )
    angle_second = (
        2.0 * math.pi / second * (index_b[:, None] * index_b[None, :] % second).astype(jnp.float32)
    )
    return (
        first,
        jnp.cos(angle_first),
        sign * jnp.sin(angle_first),
        jnp.cos(angle_twist),
        sign * jnp.sin(angle_twist),
        jnp.cos(angle_second),
        sign * jnp.sin(angle_second),
    )


def complex_section(form, real_part, imag_part, mat_cos, mat_sin):
    highest = lax.Precision.HIGHEST
    out_real = jnp.einsum(form, real_part, mat_cos, precision=highest)
    out_real = out_real - jnp.einsum(form, imag_part, mat_sin, precision=highest)
    out_imag = jnp.einsum(form, real_part, mat_sin, precision=highest)
    out_imag = out_imag + jnp.einsum(form, imag_part, mat_cos, precision=highest)
    return (out_real, out_imag)


def transform(real_part, imag_part, factors, along_last):
    first, first_cos, first_sin, twist_cos, twist_sin, second_cos, second_sin = factors
    shape = real_part.shape
    if along_last:
        blocked = (shape[0], shape[1], first, shape[2] // first)
        form_one, form_two = ("mrab,ac->mrcb", "mrcb,bd->mrdc")
        tw_cos, tw_sin = (twist_cos, twist_sin)
    else:
        blocked = (shape[0], first, shape[1] // first, shape[2])
        form_one, form_two = ("mabk,ac->mcbk", "mcbk,bd->mdck")
        tw_cos, tw_sin = (twist_cos[:, :, None], twist_sin[:, :, None])
    real_part = real_part.reshape(blocked)
    imag_part = imag_part.reshape(blocked)
    step_real, step_imag = complex_section(form_one, real_part, imag_part, first_cos, first_sin)
    twist_real = step_real * tw_cos - step_imag * tw_sin
    twist_imag = step_real * tw_sin + step_imag * tw_cos
    out_real, out_imag = complex_section(form_two, twist_real, twist_imag, second_cos, second_sin)
    out_real = out_real.reshape(shape)
    out_imag = out_imag.reshape(shape)
    return (out_real, out_imag)


def per_device(anomalies, increment, spectrum):
    col_count = anomalies.shape[2]
    row_total = spectrum.shape[0]
    forward_y = dft_tables(col_count, -1.0)
    inverse_y = dft_tables(col_count, 1.0)
    forward_x = dft_tables(row_total, -1.0)
    inverse_x = dft_tables(row_total, 1.0)
    scaled = spectrum * (1.0 / (row_total * col_count))
    fields = anomalies * increment[None]
    wave_real, wave_imag = transform(fields[0::2], fields[1::2], forward_y, True)
    part_real, part_imag = transform(
        lax.all_to_all(wave_real, "slab", split_axis=2, concat_axis=1, tiled=True),
        lax.all_to_all(wave_imag, "slab", split_axis=2, concat_axis=1, tiled=True),
        forward_x,
        False,
    )
    part_real = part_real * scaled[None]
    part_imag = part_imag * scaled[None]
    part_real, part_imag = transform(part_real, part_imag, inverse_x, False)
    back_real = lax.all_to_all(part_real, "slab", split_axis=1, concat_axis=2, tiled=True)
    back_imag = lax.all_to_all(part_imag, "slab", split_axis=1, concat_axis=2, tiled=True)
    even_part, odd_part = transform(back_real, back_imag, inverse_y, True)
    total = jnp.sum(anomalies[0::2] * even_part + anomalies[1::2] * odd_part, axis=0)
    return lax.psum(total, "mem")


def solution(mesh):
    placed = (P("mem", "slab", None), P("slab", None), P(None, "slab"))
    return jax.shard_map(
        per_device, mesh=mesh, in_specs=placed, out_specs=P("slab", None), check_vma=False
    )
```

profile of v0, /device:TPU:0, one launch (start us, length us, event | category | flops | bytes accessed | tf_op | source)
XLA Modules:
  0.0 1516.1 jit_solution(14172679125190159585)
XLA Ops:
  86.5 24.8 %fusion.6 = (f32[512,64,64]{0,1,2:T(8,128)}, f32[512,64,64]{0,1,2:T(8,128)}) fusion(f32[64,64]{0,1:T(8,128)S(1)} %get-tuple-element.17, f32[64,64]{0,1:T(8,128)S(1)} %get-tuple-element.18, f32[64,512,64]{1,0,2:T(8,128)} %fusion.69, f32[64,512,64]{1,0,2:T(8,128)} %fusion.65, f32[64,512,64]{1,0,2:T(8,128)} %fusion.67, f32[512,64,64]{0,2,1:T(8,128)} %bitcast.203), kind=kOutput, calls=%fused_computation.17 | convolution fusion | flops 1627447296 | bytes 50364416 | tf_op jit(solution)/shard_map/mrab,ac->mrcb/dot_general | solution.py:36
  111.3 16.5 %fusion.57 = f32[64,512,64]{1,0,2:T(8,128)S(1)} fusion(f32[512,64,64]{0,1,2:T(8,128)} %get-tuple-element.12), kind=kOutput, calls=%fused_computation.78 | convolution fusion | flops 1610670080 | bytes 16777216 | tf_op jit(solution)/shard_map/mrcb,bd->mrdc/dot_general | solution.py:39
  144.8 22.8 %copy.138 = f32[1,512,4096]{1,0,2:T(1,128)} copy(f32[1,512,4096]{1,2,0:T(8,128)S(1)} %bitcast.204) | data formatting | bytes 16777216 | tf_op jit(solution)/shard_map/reshape | solution.py:61
  175.2 16.3 %fusion.59 = f32[64,512,64]{1,0,2:T(8,128)S(1)} fusion(f32[512,64,64]{0,1,2:T(8,128)} %get-tuple-element.12), kind=kOutput, calls=%fused_computation.80 | convolution fusion | flops 1610674176 | bytes 16777216 | tf_op jit(solution)/shard_map/mrcb,bd->mrdc/dot_general | solution.py:37
  191.6 17.2 %subtract_bitcast_fusion.1 = f32[1,512,64,64]{1,2,3,0:T(8,128)S(1)} fusion(f32[64,512,64]{1,0,2:T(8,128)S(1)} %fusion.59, f32[512,64,64]{0,1,2:T(8,128)} %get-tuple-element.11), kind=kOutput, calls=%fused_computation.29 | convolution fusion | flops 1612767232 | bytes 25165824 | tf_op jit(solution)/shard_map/mrcb,bd->mrdc/dot_general | solution.py:36
  213.7 22.8 %copy.132 = f32[1,512,4096]{1,0,2:T(1,128)} copy(f32[1,512,4096]{1,2,0:T(8,128)S(1)} %bitcast.205) | data formatting | bytes 16777216 | tf_op jit(solution)/shard_map/reshape | solution.py:60
  236.5 121.8 %all-to-all-done.1 = f32[1,512,4096]{1,0,2:T(1,128)} async-done(((f32[1,512,4096]{1,0,2:T(1,128)}), f32[1,512,4096]{1,0,2:T(1,128)}, u32[]{:S(2)}, u32[]{:S(2)}) %all-to-all-start.1) | async-done | bytes 8388640 | tf_op jit(solution)/shard_map/all_to_all | solution.py:77
  380.4 17.8 %fusion.49 = f32[64,64,512]{2,0,1:T(8,128)} fusion(f32[64,64,512]{2,1,0:T(8,128)} %bitcast.190), kind=kOutput, calls=%fused_computation.70 | convolution fusion | flops 1610670080 | bytes 16777216 | tf_op jit(solution)/shard_map/mabk,ac->mcbk/dot_general | solution.py:39
  398.2 13.5 fusion.51
  411.7 134.0 %all-to-all-done = f32[1,512,4096]{1,0,2:T(1,128)} async-done(((f32[1,512,4096]{1,0,2:T(1,128)}), f32[1,512,4096]{1,0,2:T(1,128)}, u32[]{:S(2)}, u32[]{:S(2)}) %all-to-all-start) | async-done | bytes 8388640 | tf_op jit(solution)/shard_map/all_to_all | solution.py:76
  562.5 18.1 %fusion.55 = f32[64,64,512]{2,0,1:T(8,128)} fusion(f32[64,64,512]{2,1,0:T(8,128)} %bitcast.196), kind=kOutput, calls=%fused_computation.76 | convolution fusion | flops 1610670080 | bytes 16777216 | tf_op jit(solution)/shard_map/mabk,ac->mcbk/dot_general | solution.py:36
  580.6 24.6 %multiply_subtract_fusion.1 = (f32[64,64,512]{2,0,1:T(8,128)}, f32[64,64,512]{2,0,1:T(8,128)}) fusion(f32[64,64]{0,1:T(8,128)S(1)} %get-tuple-element.17, f32[64,64]{0,1:T(8,128)S(1)} %get-tuple-element.18, f32[64,64,512]{2,0,1:T(8,128)} %fusion.49, f32[64,64,512]{2,0,1:T(8,128)} %fusion.55, f32[64,64,512]{2,0,1:T(8,128)} %fusion.51, ...), kind=kOutput, calls=%fused_computation.27 | convolution fusion | flops 1627451392 | bytes 50364416 | tf_op jit(solution)/shard_map/mabk,ac->mcbk/dot_general | solution.py:38
  605.2 18.4 %fusion.43 = f32[64,64,512]{2,0,1:T(8,128)} fusion(f32[64,64,512]{2,0,1:T(8,128)} %get-tuple-element.10), kind=kOutput, calls=%fused_computation.64 | convolution fusion | flops 1610674176 | bytes 16777216 | tf_op jit(solution)/shard_map/mcbk,bd->mdck/dot_general | solution.py:37
  636.1 15.6 %fusion.77 = f32[64,64,512]{2,0,1:T(8,128)} fusion(f32[64,64,512]{2,0,1:T(8,128)} %fusion.43, f32[64,64,512]{2,0,1:T(8,128)S(1)} %bitcast.183), kind=kOutput, calls=%fused_computation.94 | convolution fusion | flops 1612767232 | bytes 25165824 | tf_op jit(solution)/shard_map/mcbk,bd->mdck/dot_general | solution.py:36
  663.3 13.8 fusion.80
  688.6 13.8 bitcast_multiply_fusion.6
  742.1 24.8 %multiply_subtract_fusion = (f32[64,64,512]{2,0,1:T(8,128)}, f32[64,64,512]{2,0,1:T(8,128)}) fusion(f32[64,64]{0,1:T(8,128)S(1)} %fusion.152, f32[64,64]{0,1:T(8,128)S(1)} %get-tuple-element.18, f32[64,64,512]{2,0,1:T(8,128)} %fusion.33, f32[64,64,512]{2,0,1:T(8,128)} %fusion.39, f32[64,64,512]{2,0,1:T(8,128)} %fusion.35, f32[64,64,512]{2,1,0:T(8,128)} %bitcast.186), kind=kOutput, calls=%fused_computation.25 | convolution fusion | flops 1627447296 | bytes 50364416 | tf_op jit(solution)/shard_map/mabk,ac->mcbk/dot_general | solution.py:38
  766.9 16.5 %fusion.25 = f32[64,64,512]{2,0,1:T(8,128)S(1)} fusion(f32[64,64,512]{2,0,1:T(8,128)} %get-tuple-element.8), kind=kOutput, calls=%fused_computation.46 | convolution fusion | flops 1610670080 | bytes 16777216 | tf_op jit(solution)/shard_map/mcbk,bd->mdck/dot_general | solution.py:39
  800.5 22.8 %copy.162 = f32[1,4096,512]{2,0,1:T(1,128)} copy(f32[1,4096,512]{2,1,0:T(8,128)S(1)} %bitcast.208) | data formatting | bytes 16777216 | tf_op jit(solution)/shard_map/reshape | solution.py:61
  828.5 16.3 %fusion.27 = f32[64,64,512]{2,0,1:T(8,128)S(1)} fusion(f32[64,64,512]{2,0,1:T(8,128)} %get-tuple-element.8), kind=kOutput, calls=%fused_computation.48 | convolution fusion | flops 1610670080 | bytes 16777216 | tf_op jit(solution)/shard_map/mcbk,bd->mdck/dot_general | solution.py:37
  844.8 17.2 %fusion.83 = f32[64,64,512]{2,0,1:T(8,128)S(1)} fusion(f32[64,64,512]{2,0,1:T(8,128)S(1)} %fusion.27, f32[64,64,512]{2,0,1:T(8,128)} %get-tuple-element.7), kind=kOutput, calls=%fused_computation.96 | convolution fusion | flops 1612767232 | bytes 25165824 | tf_op jit(solution)/shard_map/mcbk,bd->mdck/dot_general | solution.py:36
  866.9 22.8 %copy.156 = f32[1,4096,512]{2,0,1:T(1,128)} copy(f32[1,4096,512]{2,1,0:T(8,128)S(1)} %bitcast.209) | data formatting | bytes 16777216 | tf_op jit(solution)/shard_map/reshape | solution.py:60
  889.7 120.7 %all-to-all-done.3 = f32[1,4096,512]{2,0,1:T(1,128)} async-done(((f32[1,4096,512]{2,0,1:T(1,128)}), f32[1,4096,512]{2,0,1:T(1,128)}, u32[]{:S(2)}, u32[]{:S(2)}) %all-to-all-start.3) | async-done | bytes 8388640 | tf_op jit(solution)/shard_map/all_to_all | solution.py:85
  1032.4 17.8 %fusion.17 = f32[64,512,64]{1,0,2:T(8,128)} fusion(f32[512,64,64]{0,2,1:T(8,128)} %bitcast.192), kind=kOutput, calls=%fused_computation.38 | convolution fusion | flops 1610670080 | bytes 16777216 | tf_op jit(solution)/shard_map/mrab,ac->mrcb/dot_general | solution.py:39
  1063.5 134.1 %all-to-all-done.2 = f32[1,4096,512]{2,0,1:T(1,128)} async-done(((f32[1,4096,512]{2,0,1:T(1,128)}), f32[1,4096,512]{2,0,1:T(1,128)}, u32[]{:S(2)}, u32[]{:S(2)}) %all-to-all-start.2) | async-done | bytes 8388640 | tf_op jit(solution)/shard_map/all_to_all | solution.py:84
  1214.4 18.1 %fusion.21 = f32[64,512,64]{1,0,2:T(8,128)} fusion(f32[512,64,64]{0,2,1:T(8,128)} %bitcast.194), kind=kOutput, calls=%fused_computation.42 | convolution fusion | flops 1610670080 | bytes 16777216 | tf_op jit(solution)/shard_map/mrab,ac->mrcb/dot_general | solution.py:38
  1232.4 24.5 %fusion.2 = (f32[512,64,64]{0,1,2:T(8,128)}, f32[512,64,64]{0,1,2:T(8,128)}) fusion(f32[64,64]{0,1:T(8,128)S(1)} %fusion.152, f32[64,64]{0,1:T(8,128)S(1)} %get-tuple-element.18, f32[64,512,64]{1,0,2:T(8,128)} %fusion.21, f32[64,512,64]{1,0,2:T(8,128)} %fusion.17, f32[64,512,64]{1,0,2:T(8,128)} %fusion.19, f32[512,64,64]{0,2,1:T(8,128)} %bitcast.195), kind=kOutput, calls=%fused_computation.7 | convolution fusion | flops 1627447296 | bytes 50364416 | tf_op jit(solution)/shard_map/mrab,ac->mrcb/dot_general | solution.py:36
  1257.0 17.0 %fusion.11 = f32[64,512,64]{1,0,2:T(8,128)S(1)} fusion(f32[512,64,64]{0,1,2:T(8,128)} %get-tuple-element.6), kind=kOutput, calls=%fused_computation.32 | convolution fusion | flops 1610670080 | bytes 16777216 | tf_op jit(solution)/shard_map/mrcb,bd->mrdc/dot_general | solution.py:37
  1274.0 13.5 fusion.9
  1287.5 13.7 subtract_bitcast_fusion
  1313.0 15.6 %add_bitcast_fusion = f32[1,512,64,64]{1,2,3,0:T(8,128)} fusion(f32[64,512,64]{1,0,2:T(8,128)} %fusion.9, f32[512,64,64]{0,1,2:T(8,128)S(1)} %bitcast.181), kind=kOutput, calls=%fused_computation.22 | convolution fusion | flops 1612767232 | bytes 25165824 | tf_op jit(solution)/shard_map/mrcb,bd->mrdc/dot_general | solution.py:38
  1347.9 152.2 %all-reduce.2.cloned.1.call-done = f32[512,4096]{0,1:T(8,128)} async-done(((f32[512,4096]{0,1:T(8,128)}), f32[512,4096]{0,1:T(8,128)}) %all-reduce.2.cloned.1.call-update) | async-done | bytes 8388624 | tf_op jit(solution)/shard_map/psum | solution.py:88
  (76 shorter events, 342.5 us)
Async XLA Ops:
  46.7 26.6 %copy-start.6 = (f32[1,512,4096]{1,2,0:T(8,128)}, f32[1,512,4096]{1,2,0:T(8,128)S(1)}, u32[]{:S(2)}) copy-start(f32[1,512,4096]{1,2,0:T(8,128)S(1)} %get-tuple-element.14) | copy-start | bytes 25165828
  111.3 16.5 %copy-start = (f32[512,64,64]{0,1,2:T(8,128)S(1)}, f32[512,64,64]{0,1,2:T(8,128)}, u32[]{:S(2)}) copy-start(f32[512,64,64]{0,1,2:T(8,128)} %get-tuple-element.11) | copy-start | bytes 25165828
  167.6 190.7 %all-to-all-start.1 = ((f32[1,512,4096]{1,0,2:T(1,128)}), f32[1,512,4096]{1,0,2:T(1,128)}, u32[]{:S(2)}, u32[]{:S(2)}) async-start(f32[1,512,4096]{1,0,2:T(1,128)} %copy.138), calls=%async_computation.1 | async-start | bytes 16777216 | tf_op jit(solution)/shard_map/all_to_all | solution.py:77
  358.3 187.4 %all-to-all-start = ((f32[1,512,4096]{1,0,2:T(1,128)}), f32[1,512,4096]{1,0,2:T(1,128)}, u32[]{:S(2)}, u32[]{:S(2)}) async-start(f32[1,512,4096]{1,0,2:T(1,128)} %copy.132), calls=%async_computation | async-start | bytes 16777216 | tf_op jit(solution)/shard_map/all_to_all | solution.py:76
  380.4 17.8 %copy-start.2 = (f32[1,8,512,512]{3,2,1,0:T(8,128)S(1)}, f32[1,8,512,512]{3,2,1,0:T(8,128)}, u32[]{:S(2)}) copy-start(f32[1,8,512,512]{3,2,1,0:T(8,128)} %copy.139) | copy-start | bytes 25165828
  605.2 18.4 %copy-start.5 = (f32[64,64,512]{2,0,1:T(8,128)S(1)}, f32[64,64,512]{2,0,1:T(8,128)}, u32[]{:S(2)}) copy-start(f32[64,64,512]{2,0,1:T(8,128)} %get-tuple-element.10) | copy-start | bytes 25165828
  605.2 30.9 %slice-start.2 = ((s8[8388608]{0:T(1024)(128)(4,1)}), s8[4194304]{0:T(1024)(128)(4,1)S(1)}, s32[]{:S(2)}) async-start(s8[8388608]{0:T(1024)(128)(4,1)} %bitcast.182), calls=%async_computation.7 | async-start | bytes 8388608
  623.6 12.5 slice-start.3
  702.3 26.5 %slice-start.4 = ((s8[8388608]{0:T(1024)(128)(4,1)}), s8[4194304]{0:T(1024)(128)(4,1)S(1)}, s32[]{:S(2)}) async-start(s8[8388608]{0:T(1024)(128)(4,1)} %bitcast.187), calls=%async_computation.9 | async-start | bytes 8388608
  715.6 13.3 slice-start.5
  766.9 16.5 %copy-start.1 = (f32[64,64,512]{2,0,1:T(8,128)S(1)}, f32[64,64,512]{2,0,1:T(8,128)}, u32[]{:S(2)}) copy-start(f32[64,64,512]{2,0,1:T(8,128)} %get-tuple-element.7) | copy-start | bytes 25165828
  823.3 187.2 %all-to-all-start.3 = ((f32[1,4096,512]{2,0,1:T(1,128)}), f32[1,4096,512]{2,0,1:T(1,128)}, u32[]{:S(2)}, u32[]{:S(2)}) async-start(f32[1,4096,512]{2,0,1:T(1,128)} %copy.162), calls=%async_computation.3 | async-start | bytes 16777216 | tf_op jit(solution)/shard_map/all_to_all | solution.py:85
  1010.4 187.2 %all-to-all-start.2 = ((f32[1,4096,512]{2,0,1:T(1,128)}), f32[1,4096,512]{2,0,1:T(1,128)}, u32[]{:S(2)}, u32[]{:S(2)}) async-start(f32[1,4096,512]{2,0,1:T(1,128)} %copy.156), calls=%async_computation.2 | async-start | bytes 16777216 | tf_op jit(solution)/shard_map/all_to_all | solution.py:84
  1015.4 484.7 %all-reduce.2.cloned.1.call-start = ((), (), s32[]{:S(2)}) async-start(), calls=%async_computation.4 | async-start | bytes 16777216 | tf_op jit(solution)/shard_map/psum | solution.py:88
  1032.4 17.8 %copy-start.3 = (f32[1,512,8,512]{1,3,2,0:T(8,128)S(1)}, f32[1,512,8,512]{1,3,2,0:T(8,128)}, u32[]{:S(2)}) copy-start(f32[1,512,8,512]{1,3,2,0:T(8,128)} %copy.163) | copy-start | bytes 25165828
  1256.9 17.0 %copy-start.4 = (f32[512,64,64]{0,1,2:T(8,128)S(1)}, f32[512,64,64]{0,1,2:T(8,128)}, u32[]{:S(2)}) copy-start(f32[512,64,64]{0,1,2:T(8,128)} %get-tuple-element.6) | copy-start | bytes 25165828
  1256.9 30.6 %slice-start = ((s8[8388608]{0:T(1024)(128)(4,1)}), s8[4194304]{0:T(1024)(128)(4,1)S(1)}, s32[]{:S(2)}) async-start(s8[8388608]{0:T(1024)(128)(4,1)} %bitcast.180), calls=%async_computation.5 | async-start | bytes 8388608
  1274.0 13.5 slice-start.1
  1301.3 39.0 %slice-start.6 = ((s8[8388608]{0:T(1024)(128)(4,1)}), s8[4194304]{0:T(1024)(128)(4,1)S(1)}, s32[]{:S(2)}) async-start(s8[8388608]{0:T(1024)(128)(4,1)} %bitcast.200), calls=%async_computation.11 | async-start | bytes 8388608
  1313.0 27.3 %slice-start.7 = ((s8[8388608]{0:T(1024)(128)(4,1)}), s8[4194304]{0:T(1024)(128)(4,1)S(1)}, s32[]{:S(2)}) async-start(s8[8388608]{0:T(1024)(128)(4,1)} %bitcast.200), calls=%async_computation.12 | async-start | bytes 8388608
  1328.6 11.7 copy-start.7
Sparse Core Ops, SparseCore 0:
  1348.0 152.0 all-reduce.1
where the time goes:
time: 1520 us
  waiting for transfers between devices  663 us (44%)
  matrix products  521 us (34%)
  local copies, waits for them, and re-layouts  261 us (17%)
  other arithmetic  33.7 us (2%)
  starting transfers between devices  23 us (2%)
    psum x1, waiting for transfers between devices, per_device(): return lax.psum(total, 'mem')  152 us
    dot_general x8, matrix products, complex_section(): out_real = jnp.einsum(form, real_part, mat_cos, precision=highest)  144 us
    dot_general x8, matrix products, complex_section(): out_imag = jnp.einsum(form, real_part, mat_sin, precision=highest)  134 us
    all_to_all x1, waiting for transfers between devices, per_device(): lax.all_to_all(part_real, 'slab', split_axis=1, concat_axis=2, tiled=True)  134 us
    all_to_all x1, waiting for transfers between devices, per_device(): lax.all_to_all(wave_real, 'slab', split_axis=2, concat_axis=1, tiled=True)  134 us
    all_to_all x1, waiting for transfers between devices, per_device(): lax.all_to_all(wave_imag, 'slab', split_axis=2, concat_axis=1, tiled=True)  122 us
    dot_general x8, matrix products, complex_section(): jnp.einsum(form, imag_part, mat_sin, precision=highest)  121 us
    dot_general x8, matrix products, complex_section(): jnp.einsum(form, imag_part, mat_cos, precision=highest)  121 us
  transfers between devices with their start and end apart: 5, of which 5 were waited for; matrix products, arithmetic and copies ran while one was open for 14% of the time, Pallas kernels for 0%

commit v1 on v0

v1 whole, which is shorter than its diff:
```python
import functools
import math

import jax
import jax.numpy as jnp
import numpy as np
from jax import lax
from jax.experimental import pallas as pl
from jax.experimental.pallas import tpu as pltpu
from jax.sharding import PartitionSpec as P

LANES = 128


def butterflies(parts, sign):
    n = len(parts)
    if n == 1:
        return parts
    even = butterflies(parts[0::2], sign)
    odd = butterflies(parts[1::2], sign)
    low, high = [], []
    for k in range(n // 2):
        (er, ei), (pr, pi) = even[k], odd[k]
        if k == 0:
            tr, ti = pr, pi
        elif 4 * k == n:
            tr, ti = (pi, -pr) if sign < 0 else (-pi, pr)
        elif 8 * k == n:
            h = math.sqrt(0.5)
            tr, ti = ((pr + pi) * h, (pi - pr) * h) if sign < 0 else ((pr - pi) * h, (pr + pi) * h)
        elif 8 * k == 3 * n:
            h = math.sqrt(0.5)
            tr, ti = ((pi - pr) * h, -(pr + pi) * h) if sign < 0 else (-(pr + pi) * h, (pr - pi) * h)
        else:
            angle = sign * 2.0 * math.pi * k / n
            c, s = math.cos(angle), math.sin(angle)
            tr, ti = pr * c - pi * s, pr * s + pi * c
        low.append((er + tr, ei + ti))
        high.append((er - tr, ei - ti))
    return low + high


def split(x):
    hi = x.astype(jnp.bfloat16)
    return hi, (x - hi.astype(jnp.float32)).astype(jnp.bfloat16)


def dot(a, b):
    return jnp.dot(a, b, preferred_element_type=jnp.float32)


def lane_block(sign):
    idx = np.arange(LANES)
    angle = sign * 2.0 * np.pi / LANES * (idx[:, None] * idx[None, :] % LANES)
    c, s = np.cos(angle), np.sin(angle)
    return np.block([[c, s], [-s, c]])


def split_table(table):
    hi_np = np.asarray(table.astype(jnp.bfloat16), np.float64)
    return np.stack([table.astype(jnp.bfloat16), (table - hi_np).astype(jnp.bfloat16)])


def twist(first):
    a, b = np.arange(first), np.arange(LANES)
    angle = -2.0 * np.pi / (first * LANES) * (a[:, None] * b[None, :])
    return np.stack([np.cos(angle), np.sin(angle)]).astype(np.float32)


def exchange(tiles, group):
    lane = lax.broadcasted_iota(jnp.int32, tiles[0].shape, 1)
    step = 1
    while step * group < LANES:
        width = step * group
        upper = (lane & width) != 0
        out = list(tiles)
        for t in range(len(tiles)):
            if not t & step:
                a, b = tiles[t], tiles[t + step]
                out[t] = jnp.where(upper, pltpu.roll(b, width, 1), a)
                out[t + step] = jnp.where(upper, b, pltpu.roll(a, LANES - width, 1))
        tiles = out
        step *= 2
    return tiles


def lane_matmul(y, w_ref, rows, count):
    @pl.loop(0, count)
    def _(i):
        at = pl.ds(pl.multiple_of(i * rows, rows), rows)
        hi, lo = split(y[at, :])
        y[at, :] = dot(hi, w_ref[0]) + (dot(lo, w_ref[0]) + dot(hi, w_ref[1]))


def rows_forward(first, slabs, pieces, anom, incr, w_ref, tw, *rest):
    outs, (f, y) = rest[:pieces], rest[pieces:]
    block = incr.shape[0]
    group = LANES // slabs
    per_out = first // slabs // pieces

    @pl.loop(0, block // 16)
    def _(g):
        at = pl.ds(pl.multiple_of(g * 16, 16), 16)
        inc = incr[at, :]
        f[0, at, :] = anom[0, at, :].astype(jnp.float32) * inc
        f[1, at, :] = anom[1, at, :].astype(jnp.float32) * inc

    @pl.loop(0, block // 8)
    def _(g):
        at = pl.ds(pl.multiple_of(g * 8, 8), 8)
        parts = [
            (f[0, at, a * LANES:(a + 1) * LANES], f[1, at, a * LANES:(a + 1) * LANES])
            for a in range(first)
        ]
        for c, (r, i) in enumerate(butterflies(parts, -1.0)):
            tr, ti = tw[0, c:c + 1, :], tw[1, c:c + 1, :]
            to = pl.ds(pl.multiple_of(c * block + g * 8, 8), 8)
            y[to, :LANES] = r * tr - i * ti
            y[to, LANES:] = r * ti + i * tr

    lane_matmul(y, w_ref, 4 * block, first // 4)

    @pl.loop(0, block // 8)
    def _(g):
        at = pl.ds(pl.multiple_of(g * 8, 8), 8)
        for q in range(first // slabs):
            base = q % per_out * 2 * LANES
            for half in range(2):
                lanes = slice(half * LANES, (half + 1) * LANES)
                tiles = [
                    y[pl.ds(pl.multiple_of((q * slabs + c) * block + g * 8, 8), 8), lanes]
                    for c in range(slabs)
                ]
                for s, tile in enumerate(exchange(tiles, group)):
                    outs[q // per_out][s, at, base + half * LANES:base + (half + 1) * LANES] = tile


def rows_inverse(first, slabs, pieces, anom, w_ref, tw, *rest):
    ins, out, (f, y) = rest[:pieces], rest[pieces], rest[pieces + 1:]
    block = out.shape[0]
    group = LANES // slabs
    per_out = first // slabs // pieces

    @pl.loop(0, block // 8)
    def _(g):
        at = pl.ds(pl.multiple_of(g * 8, 8), 8)
        for q in range(first // slabs):
            base = q % per_out * 2 * LANES
            for half in range(2):
                lanes = slice(half * LANES, (half + 1) * LANES)
                tiles = [
                    ins[q // per_out][s, at, base + half * LANES:base + (half + 1) * LANES]
                    for s in range(slabs)
                ]
                for c, tile in enumerate(exchange(tiles, group)):
                    to = pl.ds(pl.multiple_of((q * slabs + c) * block + g * 8, 8), 8)
                    y[to, lanes] = tile

    lane_matmul(y, w_ref, 4 * block, first // 4)

    @pl.loop(0, block // 8)
    def _(g):
        at = pl.ds(pl.multiple_of(g * 8, 8), 8)
        parts = []
        for c in range(first):
            src = pl.ds(pl.multiple_of(c * block + g * 8, 8), 8)
            r, i = y[src, :LANES], y[src, LANES:]
            tr, ti = tw[0, c:c + 1, :], tw[1, c:c + 1, :]
            parts.append((r * tr + i * ti, i * tr - r * ti))
        for a, (r, i) in enumerate(butterflies(parts, 1.0)):
            f[0, at, a * LANES:(a + 1) * LANES] = r
            f[1, at, a * LANES:(a + 1) * LANES] = i

    @pl.loop(0, block // 16)
    def _(g):
        at = pl.ds(pl.multiple_of(g * 16, 16), 16)
        out[at, :] = anom[0, at, :].astype(jnp.float32) * f[0, at, :] + anom[1, at, :].astype(
            jnp.float32
        ) * f[1, at, :]


def columns(first, bands, x, spec, w_f, w_i, tw, *rest):
    outs, y = rest[:bands], rest[bands]
    rows = x.shape[1]
    deep = rows // bands

    @pl.loop(0, LANES // 8)
    def _(g):
        parts = []
        for a in range(first):
            s, r = divmod(a * LANES, rows)
            at = pl.ds(pl.multiple_of(r + g * 8, 8), 8)
            parts.append((x[s, at, :LANES], x[s, at, LANES:]))
        for c, (r, i) in enumerate(butterflies(parts, -1.0)):
            at = pl.ds(pl.multiple_of(g * 8, 8), 8)
            im = pl.ds(pl.multiple_of(LANES + g * 8, 8), 8)
            tr, ti = tw[0, c, at, :], tw[1, c, at, :]
            lanes = slice(c % 2 * LANES, (c % 2 + 1) * LANES)
            y[c // 2, at, lanes] = r * tr - i * ti
            y[c // 2, im, lanes] = r * ti + i * tr

    @pl.loop(0, first // 2)
    def _(p):
        hi, lo = split(y[p])
        z = dot(w_f[0], hi) + (dot(w_f[0], lo) + dot(w_f[1], hi))
        m = jnp.concatenate([spec[2 * p], spec[2 * p + 1]], axis=1)
        hi, lo = split(z * jnp.concatenate([m, m], axis=0))
        y[p] = dot(w_i[0], hi) + (dot(w_i[0], lo) + dot(w_i[1], hi))

    @pl.loop(0, LANES // 8)
    def _(g):
        at = pl.ds(pl.multiple_of(g * 8, 8), 8)
        im = pl.ds(pl.multiple_of(LANES + g * 8, 8), 8)
        parts = []
        for c in range(first):
            lanes = slice(c % 2 * LANES, (c % 2 + 1) * LANES)
            r, i = y[c // 2, at, lanes], y[c // 2, im, lanes]
            tr, ti = tw[0, c, at, :], tw[1, c, at, :]
            parts.append((r * tr + i * ti, i * tr - r * ti))
        for a, (r, i) in enumerate(butterflies(parts, 1.0)):
            s, row = divmod(a * LANES, rows)
            h, row = divmod(row, deep)
            to = pl.ds(pl.multiple_of(row + g * 8, 8), 8)
            outs[h][s, to, :LANES] = r
            outs[h][s, to, LANES:] = i


def per_device(slabs, anomalies, increment, spectrum):
    f32 = jnp.float32
    members, rows, cols = anomalies.shape
    total_rows, own = spectrum.shape
    first, first_x = cols // LANES, total_rows // LANES
    chunks = first // slabs
    pieces = 2 if chunks % 2 == 0 else 1
    per_out = chunks // pieces
    bands = max(1, min(4, rows // LANES))
    deep = rows // bands
    block = min(64, deep)
    width = per_out * 2 * LANES
    vmem = 60 * 2**20
    w_f, w_i = split_table(lane_block(-1.0)), split_table(lane_block(1.0))
    w_ft = split_table(lane_block(-1.0).T)
    w_it = split_table(lane_block(1.0).T)
    tw = twist(first)
    tw_x = jnp.broadcast_to(jnp.asarray(twist(first_x))[..., None], (2, first_x, LANES, LANES))
    group = LANES // slabs

    order = np.arange(own).reshape(group, chunks, slabs).transpose(1, 2, 0).reshape(-1)
    pick = np.zeros((own, own), np.float32)
    pick[order, np.arange(own)] = 1.0 / (total_rows * cols)
    spec = jnp.dot(spectrum, pick, precision=lax.Precision.HIGHEST)
    spec = spec.reshape(LANES, first_x, own).transpose(1, 0, 2)

    whole = lambda a: pl.BlockSpec(a.shape, lambda *_: (0,) * a.ndim)
    scratch = [pltpu.VMEM((2, block, cols), f32), pltpu.VMEM((first * block, 2 * LANES), f32)]
    params = lambda: pltpu.CompilerParams(vmem_limit_bytes=vmem)
    cost = lambda n: pl.CostEstimate(
        flops=n * 3000, bytes_accessed=n * 16, transcendentals=0
    )

    waves = pl.pallas_call(
        functools.partial(rows_forward, first, slabs, pieces),
        grid=(rows // block,),
        in_specs=[
            pl.BlockSpec((2, block, cols), lambda i: (0, i, 0)),
            pl.BlockSpec((block, cols), lambda i: (i, 0)),
            whole(w_f),
            whole(tw),
        ],
        out_specs=[pl.BlockSpec((slabs, block, width), lambda i: (0, i, 0))] * pieces,
        out_shape=[jax.ShapeDtypeStruct((slabs, rows, width), f32)] * pieces,
        scratch_shapes=scratch,
        compiler_params=params(),
        cost_estimate=cost(rows * cols),
    )(anomalies, increment, w_f, tw)

    filtered = []
    for p in range(pieces):
        got = lax.all_to_all(waves[p], "slab", 0, 0)
        filtered.append(
            pl.pallas_call(
                functools.partial(columns, first_x, bands),
                grid=(per_out,),
                in_specs=[
                    pl.BlockSpec((slabs, rows, 2 * LANES), lambda j: (0, 0, j)),
                    pl.BlockSpec((first_x, LANES, LANES), lambda j, p=p: (0, 0, p * per_out + j)),
                    whole(w_ft),
                    whole(w_it),
                    whole(tw_x),
                ],
                out_specs=[pl.BlockSpec((slabs, deep, 2 * LANES), lambda j: (0, 0, j))] * bands,
                out_shape=[jax.ShapeDtypeStruct((slabs, deep, width), f32)] * bands,
                scratch_shapes=[pltpu.VMEM((first_x // 2, 2 * LANES, 2 * LANES), f32)],
                compiler_params=params(),
                cost_estimate=cost(total_rows * width),
            )(got, spec, w_ft, w_it, tw_x)
        )

    done = []
    for h in range(bands):
        back = [lax.all_to_all(filtered[p][h], "slab", 0, 0) for p in range(pieces)]
        steps = deep // block
        part = pl.pallas_call(
            functools.partial(rows_inverse, first, slabs, pieces),
            grid=(steps,),
            in_specs=[
                pl.BlockSpec((2, block, cols), lambda i, h=h: (0, h * steps + i, 0)),
                whole(w_i),
                whole(tw),
            ]
            + [pl.BlockSpec((slabs, block, width), lambda i: (0, i, 0))] * pieces,
            out_specs=pl.BlockSpec((block, cols), lambda i: (i, 0)),
            out_shape=jax.ShapeDtypeStruct((deep, cols), f32),
            scratch_shapes=scratch,
            compiler_params=params(),
            cost_estimate=cost(deep * cols),
        )(anomalies, w_i, tw, *back)
        done.append(lax.psum(part, "mem"))
    return jnp.concatenate(done, axis=0)


def solution(mesh):
    placed = (P("mem", "slab", None), P("slab", None), P(None, "slab"))
    return jax.shard_map(
        functools.partial(per_device, mesh.shape["slab"]),
        mesh=mesh,
        in_specs=placed,
        out_specs=P("slab", None),
        check_vma=False,
    )
```

time: 1520 us -> 1030 us (0.68)
  blocking collectives: 0 us -> 501 us
  matrix products: 521 us -> 29.8 us
  waiting for transfers between devices: 663 us -> 260 us
  local copies, waits for them, and re-layouts: 261 us -> 24.6 us
  Pallas kernels: 0 us -> 185 us
  other arithmetic: 33.7 us -> 6.07 us
    all_to_all x0 -> x7, blocking collectives: none -> 501 us  [the longest x6 310 us: per_device(): back = [lax.all_to_all(filtered[p][h], 'slab', 0, 0) for p in range(pieces)]]
    dot_general x32 -> x1, matrix products: 521 us -> 29.8 us  [per_device(): spec = jnp.dot(spectrum, pick, precision=lax.Precision.HIGHEST)]
    all_to_all x4 -> x3, waiting for transfers between devices: 511 us -> 108 us  [the longest x1 92.7 us: per_device(): got = lax.all_to_all(waves[p], 'slab', 0, 0)]
    pallas_call x0 -> x7, Pallas kernels: none -> 185 us  [the longest x2 72.7 us: per_device(): pl.pallas_call(functools.partial(columns, first_x, bands), grid=(per_out,...]
    reshape x4 -> x1, local copies, waits for them, and re-layouts: 91.1 us -> 11.6 us  [per_device(): spec = spec.reshape(LANES, first_x, own).transpose(1, 0, 2)]
    unnamed x38 -> x16, local copies, waits for them, and re-layouts: 51.5 us -> 1.38 us
    all_to_all x4 -> x0, local copies, waits for them, and re-layouts: 36.8 us -> none  [the longest x1 9.35 us: per_device(): lax.all_to_all(part_imag, 'slab', split_axis=1, concat_axis=2, tiled=True)]
    add x4 -> x0, local copies, waits for them, and re-layouts: 33.3 us -> none  [complex_section(): out_imag + jnp.einsum(form, imag_part, mat_cos, precision=highest)]
  transfers between devices with their start and end apart: 5 -> 4, of which waited for: 5 -> 4; matrix products, arithmetic and copies ran while one was open for 14% -> 5% of each run, Pallas kernels for 0% -> 11%
where the time goes in v1:
time: 1030 us
  blocking collectives  501 us (49%)
  waiting for transfers between devices  260 us (25%)
  Pallas kernels  185 us (18%)
  matrix products  29.8 us (3%)
  local copies, waits for them, and re-layouts  24.6 us (2%)
  between operations  13.4 us (1%)
  starting transfers between devices  12.3 us (1%)
    all_to_all x6, blocking collectives, per_device(): back = [lax.all_to_all(filtered[p][h], 'slab', 0, 0) for p in range(pieces)]  310 us
    all_to_all x1, blocking collectives, per_device(): got = lax.all_to_all(waves[p], 'slab', 0, 0)  190 us
    psum x1, waiting for transfers between devices, per_device(): done.append(lax.psum(part, 'mem'))  152 us
    all_to_all x1, waiting for transfers between devices, per_device(): got = lax.all_to_all(waves[p], 'slab', 0, 0)  92.7 us
    pallas_call x2, Pallas kernels, per_device(): pl.pallas_call(functools.partial(columns, first_x, bands), grid=(per_out,...  72.7 us
    pallas_call x4, Pallas kernels, per_device(): pl.pallas_call(functools.partial(rows_inverse, first, slabs, pieces), gri...  58.8 us
    pallas_call x1, Pallas kernels, per_device(): pl.pallas_call(functools.partial(rows_forward, first, slabs, pieces), gri...  53.8 us
    dot_general x1, matrix products, per_device(): spec = jnp.dot(spectrum, pick, precision=lax.Precision.HIGHEST)  29.8 us
  transfers between devices with their start and end apart: 4, of which 4 were waited for; matrix products, arithmetic and copies ran while one was open for 5% of the time, Pallas kernels for 11%

profile of v1, /device:TPU:0, one launch (start us, length us, event | category | flops | bytes accessed | tf_op | source)
XLA Modules:
  0.0 1032.1 jit_solution(10192485611933045849)
XLA Ops:
  6.5 53.8 %shard_map.100 = (f32[8,512,512]{2,1,0:T(8,128)}, f32[8,512,512]{2,1,0:T(8,128)}) custom-call(bf16[2,512,4096]{2,1,0:T(8,128)(2,1)} %anom.9, f32[512,4096]{1,0:T(8,128)} %incr.1, bf16[2,256,256]{2,1,0:T(8,128)(2,1)} %constant.10.clone.w_ref.w_i, f32[2,32,128]{2,1,0:T(8,128)} %constant.8.clone.tw), custom_call_target="tpu_custom_call" | custom-call | flops 6291456000 | bytes 33554432 | tf_op jit(solution)/shard_map/pallas_call | solution.py:261
  60.3 190.4 %all_to_all.50.x = f32[8,512,512]{2,1,0:T(8,128)} all-to-all(f32[8,512,512]{2,1,0:T(8,128)} %get-tuple-element.15), channel_id=1, replica_groups=mesh['mem'=4,'slab'=8] {'slab'}, dimensions={0} | all-to-all | bytes 16777216 | tf_op jit(solution)/shard_map/all_to_all | solution.py:279
  250.7 5.1 all-to-all-start.2
  255.8 0.0 copy-done.2
  255.8 29.8 %convolution_bitcast_fusion = f32[4096,512]{0,1:T(8,128)} fusion(f32[512,512]{1,0:T(8,128)S(1)} %copy-done.2, f32[4096,512]{1,0:T(8,128)} %param.12), kind=kOutput, calls=%fused_computation.2 | convolution fusion | flops 12884901888 | bytes 17825792 | tf_op jit(solution)/shard_map/dot_general | solution.py:251
  285.7 9.0 copy.11
  294.7 11.6 %copy.14 = f32[128,32,512]{2,0,1:T(8,128)} copy(f32[128,32,512]{2,1,0:T(8,128)} %bitcast.8) | data formatting | bytes 16777216 | tf_op jit(solution)/shard_map/reshape | solution.py:252
  306.3 0.0 copy-done.7
  306.3 2.6 broadcast_in_dim.2.tw
  308.9 36.4 %shard_map.101 = (f32[8,128,512]{2,1,0:T(8,128)}, f32[8,128,512]{2,1,0:T(8,128)}, f32[8,128,512]{2,1,0:T(8,128)}, f32[8,128,512]{2,1,0:T(8,128)}) custom-call(f32[8,512,512]{2,1,0:T(8,128)} %all_to_all.50.x, f32[32,128,512]{2,1,0:T(8,128)} %bitcast.9, bf16[2,256,256]{2,1,0:T(8,128)(2,1)} %constant.11.clone.w_f.w_ref, ...), custom_call_target="tpu_custom_call" | custom-call | flops 6291456000 | bytes 33554432 | tf_op jit(solution)/shard_map/pallas_call | solution.py:281
  345.3 92.7 %all-to-all-done.2.x = f32[8,512,512]{2,1,0:T(8,128)} async-done(((f32[8,512,512]{2,1,0:T(8,128)}), f32[8,512,512]{2,1,0:T(8,128)}, u32[]{:S(2)}, u32[]{:S(2)}) %all-to-all-start.2) | async-done | bytes 8388640 | tf_op jit(solution)/shard_map/all_to_all | solution.py:279
  438.0 52.4 %all_to_all.51.rest_0_ = f32[8,128,512]{2,1,0:T(8,128)} all-to-all(f32[8,128,512]{2,1,0:T(8,128)} %get-tuple-element.16), channel_id=1, replica_groups=mesh['mem'=4,'slab'=8] {'slab'}, dimensions={0} | all-to-all | bytes 4194304 | tf_op jit(solution)/shard_map/all_to_all | solution.py:301
  490.4 51.4 %all_to_all.52.rest_0_ = f32[8,128,512]{2,1,0:T(8,128)} all-to-all(f32[8,128,512]{2,1,0:T(8,128)S(1)} %copy-done.6), channel_id=1, replica_groups=mesh['mem'=4,'slab'=8] {'slab'}, dimensions={0} | all-to-all | bytes 4194304 | tf_op jit(solution)/shard_map/all_to_all | solution.py:301
  541.8 51.3 %all_to_all.53.rest_0_ = f32[8,128,512]{2,1,0:T(8,128)} all-to-all(f32[8,128,512]{2,1,0:T(8,128)S(1)} %copy-done.5), channel_id=1, replica_groups=mesh['mem'=4,'slab'=8] {'slab'}, dimensions={0} | all-to-all | bytes 4194304 | tf_op jit(solution)/shard_map/all_to_all | solution.py:301
  593.1 3.6 all-to-all-start.8
  596.7 36.4 %shard_map.102 = (f32[8,128,512]{2,1,0:T(8,128)}, f32[8,128,512]{2,1,0:T(8,128)}, f32[8,128,512]{2,1,0:T(8,128)}, f32[8,128,512]{2,1,0:T(8,128)}) custom-call(f32[8,512,512]{2,1,0:T(8,128)} %all-to-all-done.2.x, f32[32,128,512]{2,1,0:T(8,128)} %bitcast.10, bf16[2,256,256]{2,1,0:T(8,128)(2,1)} %constant.11.clone.w_f.w_ref, ...), custom_call_target="tpu_custom_call" | custom-call | flops 6291456000 | bytes 33554432 | tf_op jit(solution)/shard_map/pallas_call | solution.py:281
  633.1 11.3 %all-to-all-done.8.rest_0_ = f32[8,128,512]{2,1,0:T(8,128)S(1)} async-done(((f32[8,128,512]{2,1,0:T(8,128)}), f32[8,128,512]{2,1,0:T(8,128)S(1)}, u32[]{:S(2)}, u32[]{:S(2)}) %all-to-all-start.8) | async-done | bytes 2097184 | tf_op jit(solution)/shard_map/all_to_all | solution.py:301
  644.4 52.5 %all_to_all.54.rest_1_ = f32[8,128,512]{2,1,0:T(8,128)} all-to-all(f32[8,128,512]{2,1,0:T(8,128)} %get-tuple-element.18), channel_id=1, replica_groups=mesh['mem'=4,'slab'=8] {'slab'}, dimensions={0} | all-to-all | bytes 4194304 | tf_op jit(solution)/shard_map/all_to_all | solution.py:301
  697.0 51.4 %all_to_all.55.rest_1_ = f32[8,128,512]{2,1,0:T(8,128)} all-to-all(f32[8,128,512]{2,1,0:T(8,128)S(1)} %copy-done.4), channel_id=1, replica_groups=mesh['mem'=4,'slab'=8] {'slab'}, dimensions={0} | all-to-all | bytes 4194304 | tf_op jit(solution)/shard_map/all_to_all | solution.py:301
  748.4 0.0 copy-done.3
  748.4 51.3 %all_to_all.56.rest_1_ = f32[8,128,512]{2,1,0:T(8,128)} all-to-all(f32[8,128,512]{2,1,0:T(8,128)S(1)} %copy-done.3), channel_id=1, replica_groups=mesh['mem'=4,'slab'=8] {'slab'}, dimensions={0} | all-to-all | bytes 4194304 | tf_op jit(solution)/shard_map/all_to_all | solution.py:301
  799.7 3.6 all-to-all-start.9
  803.3 0.0 all-reduce.3.cloned.1.call-start
  803.4 14.7 %shard_map.103 = f32[128,4096]{1,0:T(8,128)} custom-call(bf16[2,512,4096]{2,1,0:T(8,128)(2,1)} %anom.9, bf16[2,256,256]{2,1,0:T(8,128)(2,1)} %constant.11.clone.w_f.w_ref, f32[2,32,128]{2,1,0:T(8,128)} %constant.8.clone.tw, f32[8,128,512]{2,1,0:T(8,128)} %all_to_all.51.rest_0_, f32[8,128,512]{2,1,0:T(8,128)} %all_to_all.54.rest_1_), custom_call_target="tpu_custom_call" | custom-call | flops 1572864000 | bytes 8388608 | tf_op jit(solution)/shard_map/pallas_call | solution.py:303
  818.0 14.7 %shard_map.104 = f32[128,4096]{1,0:T(8,128)} custom-call(bf16[2,512,4096]{2,1,0:T(8,128)(2,1)} %anom.9, bf16[2,256,256]{2,1,0:T(8,128)(2,1)} %constant.11.clone.w_f.w_ref, f32[2,32,128]{2,1,0:T(8,128)} %constant.8.clone.tw, f32[8,128,512]{2,1,0:T(8,128)} %all_to_all.52.rest_0_, f32[8,128,512]{2,1,0:T(8,128)} %all_to_all.55.rest_1_), custom_call_target="tpu_custom_call" | custom-call | flops 1572864000 | bytes 8388608 | tf_op jit(solution)/shard_map/pallas_call | solution.py:303
  832.7 14.7 %shard_map.105 = f32[128,4096]{1,0:T(8,128)} custom-call(bf16[2,512,4096]{2,1,0:T(8,128)(2,1)} %anom.9, bf16[2,256,256]{2,1,0:T(8,128)(2,1)} %constant.11.clone.w_f.w_ref, f32[2,32,128]{2,1,0:T(8,128)} %constant.8.clone.tw, f32[8,128,512]{2,1,0:T(8,128)} %all_to_all.53.rest_0_, f32[8,128,512]{2,1,0:T(8,128)} %all_to_all.56.rest_1_), custom_call_target="tpu_custom_call" | custom-call | flops 1572864000 | bytes 8388608 | tf_op jit(solution)/shard_map/pallas_call | solution.py:303
  847.4 3.6 all-to-all-done.9.rest_1_
  851.0 1.4 copy-done.1
  852.4 14.7 %shard_map.106 = f32[128,4096]{1,0:T(8,128)} custom-call(bf16[2,512,4096]{2,1,0:T(8,128)(2,1)} %anom.9, bf16[2,256,256]{2,1,0:T(8,128)(2,1)} %constant.11.clone.w_f.w_ref, f32[2,32,128]{2,1,0:T(8,128)} %constant.8.clone.tw, f32[8,128,512]{2,1,0:T(8,128)} %copy-done, f32[8,128,512]{2,1,0:T(8,128)} %copy-done.1), custom_call_target="tpu_custom_call" | custom-call | flops 1572864000 | bytes 8388608 | tf_op jit(solution)/shard_map/pallas_call | solution.py:303
  867.1 0.0 all-reduce.3.cloned.1.call-update
  867.1 152.1 %all-reduce.3.cloned.1.call-done = (f32[128,4096]{1,0:T(8,128)}, f32[128,4096]{1,0:T(8,128)}, f32[128,4096]{1,0:T(8,128)}, f32[128,4096]{1,0:T(8,128)}) async-done(((f32[128,4096]{1,0:T(8,128)}, f32[128,4096]{1,0:T(8,128)}, f32[128,4096]{1,0:T(8,128)}, f32[128,4096]{1,0:T(8,128)}), (f32[128,4096]{1,0:T(8,128)}, f32[128,4096]{1,0:T(8,128)}, f32[128,4096]{1,0:T(8,128)}, ...) | async-done | bytes 8388624 | tf_op jit(solution)/shard_map/psum | solution.py:318
  1019.2 6.1 pad_maximum_fusion
  (12 shorter events, 0.0 us)
Async XLA Ops:
  250.7 5.1 copy-start.2
  250.7 187.3 %all-to-all-start.2 = ((f32[8,512,512]{2,1,0:T(8,128)}), f32[8,512,512]{2,1,0:T(8,128)}, u32[]{:S(2)}, u32[]{:S(2)}) async-start(f32[8,512,512]{2,1,0:T(8,128)} %get-tuple-element.17), calls=%async_computation.2 | async-start | bytes 16777216 | tf_op jit(solution)/shard_map/all_to_all | solution.py:279
  294.7 11.6 %copy-start.7 = (f32[2,32,128]{2,1,0:T(8,128)S(1)}, f32[2,32,128]{2,1,0:T(8,128)}, u32[]{:S(2)}) copy-start(f32[2,32,128]{2,1,0:T(8,128)} %constant.8.clone.tw) | copy-start | bytes 98308
  438.0 52.4 %copy-start.6 = (f32[8,128,512]{2,1,0:T(8,128)S(1)}, f32[8,128,512]{2,1,0:T(8,128)}, u32[]{:S(2)}) copy-start(f32[8,128,512]{2,1,0:T(8,128)} %get-tuple-element.19) | copy-start | bytes 6291460
  490.4 51.4 %copy-start.5 = (f32[8,128,512]{2,1,0:T(8,128)S(1)}, f32[8,128,512]{2,1,0:T(8,128)}, u32[]{:S(2)}) copy-start(f32[8,128,512]{2,1,0:T(8,128)} %get-tuple-element.21) | copy-start | bytes 6291460
  593.1 51.3 %all-to-all-start.8 = ((f32[8,128,512]{2,1,0:T(8,128)}), f32[8,128,512]{2,1,0:T(8,128)S(1)}, u32[]{:S(2)}, u32[]{:S(2)}) async-start(f32[8,128,512]{2,1,0:T(8,128)} %get-tuple-element.23), calls=%async_computation.8 | async-start | bytes 4194304 | tf_op jit(solution)/shard_map/all_to_all | solution.py:301
  644.4 52.5 %copy-start = (f32[8,128,512]{2,1,0:T(8,128)}, f32[8,128,512]{2,1,0:T(8,128)S(1)}, u32[]{:S(2)}) copy-start(f32[8,128,512]{2,1,0:T(8,128)S(1)} %all-to-all-done.8.rest_0_) | copy-start | bytes 6291460
  644.4 52.5 %copy-start.4 = (f32[8,128,512]{2,1,0:T(8,128)S(1)}, f32[8,128,512]{2,1,0:T(8,128)}, u32[]{:S(2)}) copy-start(f32[8,128,512]{2,1,0:T(8,128)} %get-tuple-element.20) | copy-start | bytes 6291460
  697.0 51.4 %copy-start.3 = (f32[8,128,512]{2,1,0:T(8,128)S(1)}, f32[8,128,512]{2,1,0:T(8,128)}, u32[]{:S(2)}) copy-start(f32[8,128,512]{2,1,0:T(8,128)} %get-tuple-element.22) | copy-start | bytes 6291460
  799.7 51.3 %all-to-all-start.9 = ((f32[8,128,512]{2,1,0:T(8,128)}), f32[8,128,512]{2,1,0:T(8,128)S(1)}, u32[]{:S(2)}, u32[]{:S(2)}) async-start(f32[8,128,512]{2,1,0:T(8,128)} %get-tuple-element.24), calls=%async_computation.9 | async-start | bytes 4194304 | tf_op jit(solution)/shard_map/all_to_all | solution.py:301
  803.3 215.9 %all-reduce.3.cloned.1.call-start = ((), (), s32[]{:S(2)}) async-start(), calls=%async_computation.10 | async-start | bytes 16777216 | tf_op jit(solution)/shard_map/psum | solution.py:318
  851.0 1.4 copy-start.1
Sparse Core Ops, SparseCore 0:
  867.2 151.9 all-reduce.2
